TPU v7x, 128 devices: a whole 4x4x4 slice. The times are simulated.
128 devices in a mesh: cp: 32 (over z, y, x_lo), fsdp: 4 (over x_hi, core).
Axes of the slice: x: 4 (x_hi: 2, x_lo: 2; x = x_hi * 2 + x_lo), y: 4, z: 4, core: 2. Of those that a mesh axis runs over, the one named last changes fastest.
Arguments:
- query_states: bfloat16 [4, 4096, 1024], P('fsdp', 'cp'), may hold values from -32 to 32
- key_states: bfloat16 [4, 4096, 1024], P('fsdp', 'cp'), may hold values from -32 to 32
- value_states: bfloat16 [4, 4096, 1024], P('fsdp', 'cp'), may hold values from -6 to 6
- span_order: int32 [64], replicated, may hold values from 0 to 63, as said below
- block_mask: int32 [64, 64], replicated, may hold values from 0 to 1, as said below
- output_weight: bfloat16 [1024, 2048], P(('cp', 'fsdp')), may hold values from -0.1875 to 0.1875
- upstream: bfloat16 [4, 4096, 2048], P('fsdp', 'cp'), may hold values from -6 to 6
Outputs:
- projected: bfloat16 [4, 4096, 2048], P('fsdp', 'cp')
- query_gradient: bfloat16 [4, 4096, 1024], P('fsdp', 'cp')
- key_gradient: bfloat16 [4, 4096, 1024], P('fsdp', 'cp')
- value_gradient: bfloat16 [4, 4096, 1024], P('fsdp', 'cp')
- weight_gradient: float32 [1024, 2048], P(('cp', 'fsdp'))
Inputs may be any that keep to these rules, and one draw needn't show every extreme that they name: `span_order`: entries 2 d and 2 d + 1 hold positions p and 63 - p; every position appears once. `block_mask`: the diagonal is 1.
All inputs are finite; a program needn't handle non-finite values.
Results may differ from a plain program's by a relative error of at most 0.024.
Values may be sent and summed in bfloat16 or wider, within the bound.
No kernel may reach another device: no remote copies, remote signals or barrier semaphores. Data moves between devices by JAX's collectives and lax.ppermute only.
A program may use at most 128 MiB of HBM per device.

v0:
```python
import math
import jax
import jax.numpy as jnp
from jax import lax
from jax.sharding import PartitionSpec as P

HEADS = 8
HEAD = 128
lowest = -1e30


def side_by_side(arrays, axis, dim, along):
    widths = [a.shape[along] for a in arrays]
    both = jnp.concatenate(arrays, axis=along)
    filled = lax.all_gather(both, axis, axis=dim, tiled=True)
    return tuple(jnp.split(filled, [sum(widths[:k]) for k in range(1, len(widths))], axis=along))


def cut_along(array, dim, size):
    before, after = (array.shape[:dim], array.shape[dim + 1 :])
    return jnp.moveaxis(array.reshape(*before, size, -1, *after), dim, 0)


def summed_on_arrival(array, axis, dim):
    size = lax.axis_size(axis)
    tiles = lax.all_to_all(cut_along(array, dim, size), axis, 0, 0, tiled=True)
    return jnp.sum(tiles.astype(jnp.float32), axis=0)


def split_heads(row_block):
    return row_block.reshape(row_block.shape[0], HEADS, HEAD)


def pair_scores(query_rows, key_rows):
    return jnp.einsum(
        "qhd,khd->hqk",
        split_heads(query_rows),
        split_heads(key_rows),
        preferred_element_type=jnp.float32,
    ) * (1.0 / HEAD)


def storage_mask(span_order, block_mask):
    span_count = span_order.shape[0]
    onehot = (span_order[:, None] == jnp.arange(span_count, dtype=jnp.int32)[None, :]).astype(
        jnp.float32
    )
    permuted = jnp.dot(jnp.dot(onehot, block_mask.astype(jnp.float32)), onehot.T)
    return permuted > 0.5


def allowed_block(span_ok, positions, query_begin, query_total, key_begin, key_total, span_rows):
    span_sub = lax.dynamic_slice(
        span_ok,
        (query_begin // span_rows, key_begin // span_rows),
        (query_total // span_rows, key_total // span_rows),
    )
    spread = jnp.broadcast_to(
        span_sub[:, None, :, None],
        (query_total // span_rows, span_rows, key_total // span_rows, span_rows),
    )
    spread = spread.reshape(query_total, key_total)
    query_pos = lax.dynamic_slice_in_dim(positions, query_begin, query_total)
    key_pos = lax.dynamic_slice_in_dim(positions, key_begin, key_total)
    return spread & (key_pos[None, :] <= query_pos[:, None])


def local_terms(query_rows, grad_rows, log_rows, delta_rows, key_rows, value_rows, allowed):
    scores = pair_scores(query_rows, key_rows)
    probability = jnp.where(allowed[None], jnp.exp(scores - log_rows[..., None]), 0.0)
    dprob = jnp.einsum(
        "qhd,khd->hqk",
        split_heads(grad_rows),
        split_heads(value_rows),
        preferred_element_type=jnp.float32,
    )
    dscores = (probability * (dprob - delta_rows[..., None]) * (1.0 / HEAD)).astype(jnp.bfloat16)
    return (probability, dscores)


def local(query_states, key_states, value_states, span_order, block_mask, output_weight, upstream):
    query_rows = query_states[0]
    key_local = key_states[0]
    value_local = value_states[0]
    upstream_rows = upstream[0]
    tokens = query_rows.shape[0]
    span_rows = tokens // 2
    positions = (
        span_order[:, None] * span_rows + jnp.arange(span_rows, dtype=jnp.int32)[None, :]
    ).reshape(-1)
    span_ok = storage_mask(span_order, block_mask)
    own_start = lax.axis_index("cp") * tokens
    key_all, value_all = side_by_side((key_local, value_local), "cp", 0, 1)
    weight = lax.all_gather(output_weight, ("cp", "fsdp"), axis=0, tiled=True)
    length = key_all.shape[0]
    key_block = math.gcd(length, 512)
    block_count = length // key_block
    block_steps = jnp.arange(block_count, dtype=jnp.int32)

    def stats_step(running, step_index):
        key_begin = step_index * key_block
        key_rows = lax.dynamic_slice_in_dim(key_all, key_begin, key_block)
        allowed = allowed_block(
            span_ok, positions, own_start, tokens, key_begin, key_block, span_rows
        )
        maxima, totals = running
        scores = pair_scores(query_rows, key_rows)
        masked = jnp.where(allowed[None], scores, lowest)
        new_max = jnp.maximum(maxima, masked.max(-1))
        exp_terms = jnp.where(allowed[None], jnp.exp(scores - new_max[..., None]), 0.0)
        return ((new_max, totals * jnp.exp(maxima - new_max) + exp_terms.sum(-1)), None)

    stat_start = (
        jnp.full((HEADS, tokens), lowest, jnp.float32),
        jnp.zeros((HEADS, tokens), jnp.float32),
    )
    (maxima, totals), _ = lax.scan(stats_step, stat_start, block_steps)
    log_total = maxima + jnp.log(totals)

    def output_step(attn_sum, step_index):
        key_begin = step_index * key_block
        key_rows = lax.dynamic_slice_in_dim(key_all, key_begin, key_block)
        value_rows = lax.dynamic_slice_in_dim(value_all, key_begin, key_block)
        allowed = allowed_block(
            span_ok, positions, own_start, tokens, key_begin, key_block, span_rows
        )
        scores = pair_scores(query_rows, key_rows)
        probability = jnp.where(allowed[None], jnp.exp(scores - log_total[..., None]), 0.0)
        return (
            attn_sum
            + jnp.einsum(
                "hqk,khd->qhd",
                probability.astype(jnp.bfloat16),
                split_heads(value_rows),
                preferred_element_type=jnp.float32,
            ),
            None,
        )

    zero_heads = jnp.zeros((tokens, HEADS, HEAD), jnp.float32)
    attn_sum, _ = lax.scan(output_step, zero_heads, block_steps)
    attended = lax.optimization_barrier(attn_sum.reshape(tokens, -1).astype(jnp.bfloat16))
    projected = jnp.dot(attended, weight, preferred_element_type=jnp.float32).astype(jnp.bfloat16)
    grad_attended = lax.dot_general(
        upstream_rows, weight, (((1,), (1,)), ((), ())), preferred_element_type=jnp.float32
    ).astype(jnp.bfloat16)
    grad_attended = lax.optimization_barrier(grad_attended)
    weight_term = lax.dot_general(
        attended, upstream_rows, (((0,), (0,)), ((), ())), preferred_element_type=jnp.float32
    )
    row_delta = (
        (grad_attended.astype(jnp.float32) * attended.astype(jnp.float32))
        .reshape(tokens, HEADS, HEAD)
        .sum(-1)
    )
    delta_heads = row_delta.T

    def query_step(grad_sum, step_index):
        key_begin = step_index * key_block
        key_rows = lax.dynamic_slice_in_dim(key_all, key_begin, key_block)
        value_rows = lax.dynamic_slice_in_dim(value_all, key_begin, key_block)
        allowed = allowed_block(
            span_ok, positions, own_start, tokens, key_begin, key_block, span_rows
        )
        probability, dscores = local_terms(
            query_rows, grad_attended, log_total, delta_heads, key_rows, value_rows, allowed
        )
        return (
            grad_sum
            + jnp.einsum(
                "hqk,khd->qhd", dscores, split_heads(key_rows), preferred_element_type=jnp.float32
            ),
            None,
        )

    query_sum, _ = lax.scan(query_step, zero_heads, block_steps)
    query_gradient = query_sum.reshape(tokens, -1).astype(jnp.bfloat16)
    log_all, delta_all = side_by_side((log_total.T, row_delta), "cp", 0, 1)
    sums_now = (zero_heads, zero_heads)
    query_piece, grad_piece = side_by_side((query_rows, grad_attended), "cp", 0, 1)
    row_count = query_piece.shape[0]
    sources = row_count // tokens
    group_size = math.gcd(sources, max(1, 512 // tokens))
    group_rows = group_size * tokens

    def group_step(running, step_index):
        offset = step_index * group_rows
        query_group = lax.dynamic_slice_in_dim(query_piece, offset, group_rows)
        grad_group = lax.dynamic_slice_in_dim(grad_piece, offset, group_rows)
        log_group = lax.dynamic_slice_in_dim(log_all, offset, group_rows).T
        delta_group = lax.dynamic_slice_in_dim(delta_all, offset, group_rows).T
        allowed = allowed_block(
            span_ok, positions, offset, group_rows, own_start, tokens, span_rows
        )
        key_sum, value_sum = running
        probability, dscores = local_terms(
            query_group, grad_group, log_group, delta_group, key_local, value_local, allowed
        )
        probability_low = probability.astype(jnp.bfloat16).reshape(
            HEADS, group_size, tokens, tokens
        )
        dscores_group = dscores.reshape(HEADS, group_size, tokens, tokens)
        qsplit = query_group.reshape(group_size, tokens, HEADS, HEAD)
        gsplit = grad_group.reshape(group_size, tokens, HEADS, HEAD)
        key_part = jnp.einsum(
            "hgqk,gqhd->gkhd", dscores_group, qsplit, preferred_element_type=jnp.float32
        ).astype(jnp.bfloat16)
        value_part = jnp.einsum(
            "hgqk,gqhd->gkhd", probability_low, gsplit, preferred_element_type=jnp.float32
        ).astype(jnp.bfloat16)
        key_part, value_part = lax.optimization_barrier((key_part, value_part))
        return (
            (
                key_sum + key_part.astype(jnp.float32).sum(0),
                value_sum + value_part.astype(jnp.float32).sum(0),
            ),
            None,
        )

    sums_now, _ = lax.scan(group_step, sums_now, jnp.arange(sources // group_size, dtype=jnp.int32))
    key_sum, value_sum = sums_now
    key_gradient = key_sum.reshape(tokens, -1).astype(jnp.bfloat16)
    value_gradient = value_sum.reshape(tokens, -1).astype(jnp.bfloat16)
    cycle_count = lax.axis_size("cp")
    batch_count = lax.axis_size("fsdp")
    slab_rows = weight_term.shape[0] // (cycle_count * batch_count)
    reordered = weight_term.reshape(cycle_count, batch_count, slab_rows, -1).transpose(1, 0, 2, 3)
    reordered = reordered.reshape(weight_term.shape[0], -1)
    partial_batch = summed_on_arrival(reordered.astype(jnp.bfloat16), "fsdp", 0)
    weight_gradient = summed_on_arrival(partial_batch.astype(jnp.bfloat16), "cp", 0)
    return (
        projected[None],
        query_gradient[None],
        key_gradient[None],
        value_gradient[None],
        weight_gradient,
    )


def solution(mesh):
    return jax.shard_map(
        local,
        mesh=mesh,
        in_specs=(
            P("fsdp", "cp", None),
            P("fsdp", "cp", None),
            P("fsdp", "cp", None),
            P(),
            P(),
            P(("cp", "fsdp"), None),
            P("fsdp", "cp", None),
        ),
        out_specs=(
            P("fsdp", "cp", None),
            P("fsdp", "cp", None),
            P("fsdp", "cp", None),
            P("fsdp", "cp", None),
            P(("cp", "fsdp"), None),
        ),
        check_vma=False,
    )
```

profile of v0, /device:TPU:1, one launch (start us, length us, event | category | flops | bytes accessed | tf_op | source)
XLA Modules:
  0.0 1168.4 jit_solution(7732555768528166424)
XLA Ops:
  11.1 199.5 %all-gather.6.cloned.1.call-done = bf16[1024,2048]{1,0:T(8,128)(2,1)} async-done(((bf16[8,2048]{1,0:T(8,128)(2,1)}), bf16[1024,2048]{1,0:T(8,128)(2,1)}) %all-gather.6.cloned.1.call-update) | async-done | bytes 4194320 | tf_op jit(solution)/shard_map/all_gather | solution.py:94
  210.6 3.7 convolution_convert_fusion.3
  215.9 354.4 %all-gather.4.cloned.1.call-done = bf16[4096,2048]{0,1:T(8,128)(2,1)} async-done(((bf16[128,2048]{0,1:T(8,128)(2,1)}), bf16[4096,2048]{0,1:T(8,128)(2,1)}) %all-gather.4.cloned.1.call-update) | async-done | bytes 16777232 | tf_op jit(solution)/shard_map/all_gather | solution.py:15
  570.3 11.8 %fusion.61 = (bf16[4096,1024]{0,1:T(8,128)(2,1)}, bf16[4096,1024]{0,1:T(8,128)(2,1)}) fusion(bf16[4096,2048]{0,1:T(8,128)(2,1)} %all-gather.4.cloned.1.call-done), kind=kLoop, calls=%fused_computation.94 | loop fusion | bytes 33554432 | tf_op jit(solution)/shard_map/split | solution.py:16
  582.1 36.4 %while.60 = (s32[]{:T(128)}, f32[8,128]{1,0:T(8,128)S(1)}, f32[8,128]{1,0:T(8,128)S(1)}, s32[8]{0:T(128)S(1)}, pred[64,64]{1,0:T(8,128)(4,1)S(1)}, /*index=5*/s3...) while((s32[]{:T(128)}, f32[8,128]{1,0:T(8,128)S(1)}, ...), condition=%wide.region_3.4_spmd.clone, body=%wide.region_0.3_spmd.clone.sunk | while | flops 138023952 | bytes 8776669 | solution.py:117
  618.5 51.7 %while.61 = (s32[]{:T(128)}, f32[128,8,128]{0,2,1:T(8,128)}, s32[8]{0:T(128)S(1)}, bf16[4096,1024]{0,1:T(8,128)(2,1)}, pred[64,64]{1,0:T(8,128)(4,1)S(1)}, /*ind...) while((s32[]{:T(128)}, f32[128,8,128]{0,2,1:T(8,128)}, ...), condition=%wide.region_5.6_spmd.clone, body=%wide.region_4.5_spmd.clone.sunk | while | flops 270925856 | bytes 8661988 | solution.py:141
  675.6 5.5 all-to-all-start
  681.2 75.2 %while.62 = (s32[]{:T(128)}, f32[128,8,128]{0,2,1:T(8,128)}, s32[8]{0:T(128)S(1)}, bf16[4096,1024]{0,1:T(8,128)(2,1)}, pred[64,64]{1,0:T(8,128)(4,1)S(1)}, /*ind...) while((s32[]{:T(128)}, f32[128,8,128]{0,2,1:T(8,128)}, ...), condition=%wide.region_8.9_spmd.clone, body=%wide.region_7.8_spmd.clone.sunk | while | flops 406716416 | bytes 14171124 | solution.py:176
  686.9 3.6 fusion.117
  696.2 3.7 fusion.117
  705.6 3.7 fusion.117
  715.0 3.7 fusion.117
  724.4 3.7 fusion.117
  733.8 3.7 fusion.117
  743.2 3.7 fusion.117
  752.6 3.7 fusion.117
  758.3 3.7 fusion.46
  762.0 13.3 %all-to-all-done = bf16[4,256,2048]{2,1,0:T(8,128)(2,1)} async-done(((bf16[4,256,2048]{2,1,0:T(8,128)(2,1)}), bf16[4,256,2048]{2,1,0:T(8,128)(2,1)}, u32[]{:S(2)}, u32[]{:S(2)}) %all-to-all-start) | async-done | bytes 4194336 | tf_op jit(solution)/shard_map/all_to_all | solution.py:26
  775.3 4.3 reduce_sum.70
  779.5 7.7 all-to-all-start.1
  787.3 94.1 %all_gather.15 = f32[4096,16]{0,1:T(8,128)S(1)} all-gather(f32[128,16]{0,1:T(8,128)S(1)} %pad_maximum_fusion.2), channel_id=1, replica_groups=mesh['cp'=32,'fsdp'=4] {'cp'}, dimensions={0}, use_global_device_ids=true | all-gather | bytes 270336 | tf_op jit(solution)/shard_map/all_gather | solution.py:15
  882.9 115.3 %all-gather.8.cloned.1.call-done = bf16[4096,2048]{1,0:T(8,128)(2,1)} async-done(((bf16[128,2048]{1,0:T(8,128)(2,1)}), bf16[4096,2048]{1,0:T(8,128)(2,1)}) %all-gather.8.cloned.1.call-update) | async-done | bytes 16777232 | tf_op jit(solution)/shard_map/all_gather | solution.py:15
  998.1 11.6 fusion.60
  1009.8 148.1 %while.63 = (s32[]{:T(128)}, f32[128,8,128]{0,2,1:T(8,128)}, f32[128,8,128]{0,2,1:T(8,128)}, s32[8]{0:T(128)S(1)}, bf16[4096,1024]{1,0:T(8,128)(2,1)}, /*index=5...) while((s32[]{:T(128)}, f32[128,8,128]{0,2,1:T(8,128)}, ...), condition=%wide.region_12.13_spmd.clone, body=%wide.region_9.12_spmd.clone.sunk | while | flops 544604160 | bytes 55680292 | solution.py:220
  (683 shorter events, 276.1 us)
Async XLA Ops:
  7.2 203.4 %copy-start = (bf16[1,128,2048]{2,1,0:T(8,128)(2,1)S(1)}, bf16[1,128,2048]{2,1,0:T(8,128)(2,1)}, u32[]{:S(2)}) copy-start(bf16[1,128,2048]{2,1,0:T(8,128)(2,1)} %param.21) | copy-start | bytes 1572868
  7.2 203.4 %all-gather.6.cloned.1.call-start = ((), (), s32[]{:S(2)}) async-start(), calls=%async_computation.3 | async-start | bytes 4227072 | tf_op jit(solution)/shard_map/all_gather | solution.py:94
  7.9 562.4 %all-gather.4.cloned.1.call-start = ((), (), s32[]{:S(2)}) async-start(), calls=%async_computation.2 | async-start | bytes 17301504 | tf_op jit(solution)/shard_map/all_gather | solution.py:15
  11.1 203.3 %copy-start.4 = (bf16[1,128,1024]{2,1,0:T(8,128)(2,1)S(1)}, bf16[1,128,1024]{2,1,0:T(8,128)(2,1)}, u32[]{:S(2)}) copy-start(bf16[1,128,1024]{2,1,0:T(8,128)(2,1)} %param.15) | copy-start | bytes 786436
  11.1 204.2 %copy-start.15 = (s32[64]{0:T(128)S(1)}, s32[64]{0:T(128)}, u32[]{:S(2)}) copy-start(s32[64]{0:T(128)} %param.18) | copy-start | bytes 772
  11.1 204.3 %copy-start.14 = (s32[64,64]{1,0:T(8,128)S(1)}, s32[64,64]{1,0:T(8,128)}, u32[]{:S(2)}) copy-start(s32[64,64]{1,0:T(8,128)} %param.19) | copy-start | bytes 49156
  11.1 987.0 %all-gather.8.cloned.1.call-start = ((), (), s32[]{:S(2)}) async-start(), calls=%async_computation.4 | async-start | bytes 17301504 | tf_op jit(solution)/shard_map/all_gather | solution.py:15
  675.6 99.6 %all-to-all-start = ((bf16[4,256,2048]{2,1,0:T(8,128)(2,1)}), bf16[4,256,2048]{2,1,0:T(8,128)(2,1)}, u32[]{:S(2)}, u32[]{:S(2)}) async-start(bf16[4,256,2048]{2,1,0:T(8,128)(2,1)} %bitcast.259), calls=%async_computation | async-start | bytes 8388608 | tf_op jit(solution)/shard_map/all_to_all | solution.py:26
  779.5 102.5 %all-to-all-start.1 = ((bf16[32,8,2048]{2,1,0:T(8,128)(2,1)}), bf16[32,8,2048]{2,1,0:T(8,128)(2,1)S(1)}, u32[]{:S(2)}, u32[]{:S(2)}) async-start(bf16[32,8,2048]{2,1,0:T(8,128)(2,1)} %bitcast.17), calls=%async_computation.1 | async-start | bytes 2097152 | tf_op jit(solution)/shard_map/all_to_all | solution.py:26
  882.9 126.9 %copy-start.10 = (bf16[1,128,1024]{2,1,0:T(8,128)(2,1)S(1)}, bf16[1,128,1024]{2,1,0:T(8,128)(2,1)}, u32[]{:S(2)}) copy-start(bf16[1,128,1024]{2,1,0:T(8,128)(2,1)} %param.16) | copy-start | bytes 786436
  1009.8 4.2 copy-start.12
  1016.7 4.5 copy-start.9
  1028.3 4.1 copy-start.12
  1035.2 4.5 copy-start.9
  1046.8 4.1 copy-start.12
  1053.7 4.5 copy-start.9
  1065.4 4.1 copy-start.12
  1072.3 4.5 copy-start.9
  1083.9 4.1 copy-start.12
  1090.8 4.5 copy-start.9
  1102.4 4.1 copy-start.12
  1109.3 4.5 copy-start.9
  1127.8 4.5 copy-start.9
  1146.3 4.5 copy-start.9
  (67 other events, 101.7 us)
Sparse Core Ops, SparseCore 0:
  9.7 200.8 all-gather.5
  212.2 358.1 all-gather.3
  572.0 426.1 all-gather.7
where the time goes:
time: 1170 us
  waiting for transfers between devices  683 us (58%)
  local copies, waits for them, and re-layouts  196 us (17%)
  matrix products  119 us (10%)
  blocking collectives  94.1 us (8%)
  other arithmetic  24.1 us (2%)
  loops' own time  23.7 us (2%)
  between operations  14 us (1%)
  starting transfers between devices  13.4 us (1%)
    all_gather x2, waiting for transfers between devices, side_by_side(): filled = lax.all_gather(both, axis, axis=dim, tiled=True)  470 us
    all_gather x1, waiting for transfers between devices, local(): weight = lax.all_gather(output_weight, ('cp', 'fsdp'), axis=0, tiled=True)  199 us
    all_gather x1, blocking collectives, side_by_side(): filled = lax.all_gather(both, axis, axis=dim, tiled=True)  94.1 us
    dot_general x24, matrix products, pair_scores(): jnp.einsum('qhd,khd->hqk', split_heads(query_rows), split_heads(key_rows)...  34.9 us
    dynamic_slice x16, local copies, waits for them, and re-layouts, group_step(): grad_group = lax.dynamic_slice_in_dim(grad_piece, offset, group_rows)  30.5 us
    dot_general x8, matrix products, query_step(): jnp.einsum('hqk,khd->qhd', dscores, split_heads(key_rows), preferred_elem...  29.7 us
    split x3, local copies, waits for them, and re-layouts, side_by_side(): jnp.split(filled, [sum(widths[:k]) for k in range(1, len(widths))], axis=...  24.1 us
  transfers between devices with their start and end apart: 5, of which 4 were waited for; matrix products, arithmetic and copies ran while one was open for 16% of the time, Pallas kernels for 0%

commit v1 on v0

--- a/solution.py
+++ b/solution.py
@@ -91,7 +91,15 @@
     span_ok = storage_mask(span_order, block_mask)
     own_start = lax.axis_index("cp") * tokens
     key_all, value_all = side_by_side((key_local, value_local), "cp", 0, 1)
-    weight = lax.all_gather(output_weight, ("cp", "fsdp"), axis=0, tiled=True)
+    weight = jnp.concatenate(
+        lax.all_to_all(
+            jnp.stack([output_weight for _ in range(lax.axis_size(("cp", "fsdp")))]),
+            axis_name=("cp", "fsdp"),
+            split_axis=0,
+            concat_axis=0,
+        ),
+        axis=0,
+    )
     length = key_all.shape[0]
     key_block = math.gcd(length, 512)
     block_count = length // key_block

time: 1170 us -> 1020 us (0.87)
  waiting for transfers between devices: 683 us -> 420 us
  blocking collectives: 94.1 us -> 187 us
  local copies, waits for them, and re-layouts: 196 us -> 227 us
  matrix products: 119 us -> 96.2 us
    all_gather x1 -> x0, waiting for transfers between devices: 199 us -> none  [local(): weight = lax.all_gather(output_weight, ('cp', 'fsdp'), axis=0, tiled=True)]
    all_to_all x0 -> x1, blocking collectives: none -> 109 us  [local(): lax.all_to_all(jnp.stack([output_weight for _ in range(lax.axis_size(('cp...]
    all_gather x2, waiting for transfers between devices: 470 us -> 420 us  [side_by_side(): filled = lax.all_gather(both, axis, axis=dim, tiled=True)]
    all_gather x1, blocking collectives: 94.1 us -> 77.4 us  [side_by_side(): filled = lax.all_gather(both, axis, axis=dim, tiled=True)]
    dynamic_slice x24, local copies, waits for them, and re-layouts: 1.9 us -> 18.2 us  [allowed_block(): key_pos = lax.dynamic_slice_in_dim(positions, key_begin, key_total)]
    dynamic_slice x16, local copies, waits for them, and re-layouts: 30.5 us -> 14.8 us  [group_step(): grad_group = lax.dynamic_slice_in_dim(grad_piece, offset, group_rows)]
    all_to_all x2, waiting for transfers between devices: 13.3 us -> 0.01 us  [summed_on_arrival(): tiles = lax.all_to_all(cut_along(array, dim, size), axis, 0, 0, tiled=True)]
    while x208, local copies, waits for them, and re-layouts: 17.8 us -> 30.7 us
  transfers between devices with their start and end apart: 5 -> 4, of which waited for: 4 -> 2; matrix products, arithmetic and copies ran while one was open for 16% -> 32% of each run, Pallas kernels for 0% -> 0%
where the time goes in v1:
time: 1020 us; the launch traced here: 1010 us
  waiting for transfers between devices  420 us (41%)
  local copies, waits for them, and re-layouts  227 us (22%)
  blocking collectives  187 us (18%)
  matrix products  96.2 us (9%)
  other arithmetic  27.4 us (3%)
  loops' own time  24.7 us (2%)
  between operations  14.3 us (1%)
  starting transfers between devices  13.2 us (1%)
    all_gather x2, waiting for transfers between devices, side_by_side(): filled = lax.all_gather(both, axis, axis=dim, tiled=True)  420 us
    all_to_all x1, blocking collectives, local(): lax.all_to_all(jnp.stack([output_weight for _ in range(lax.axis_size(('cp...  109 us
    all_gather x1, blocking collectives, side_by_side(): filled = lax.all_gather(both, axis, axis=dim, tiled=True)  77.4 us
    while x208, local copies, waits for them, and re-layouts  30.7 us
    dot_general x8, matrix products, query_step(): jnp.einsum('hqk,khd->qhd', dscores, split_heads(key_rows), preferred_elem...  27.8 us
    dynamic_slice x32, local copies, waits for them, and re-layouts, local(): (maxima, totals), _ = lax.scan(stats_step, stat_start, block_steps)  24.7 us
    dot_general x24, matrix products, pair_scores(): jnp.einsum('qhd,khd->hqk', split_heads(query_rows), split_heads(key_rows)...  23.9 us
    split x3, local copies, waits for them, and re-layouts, side_by_side(): jnp.split(filled, [sum(widths[:k]) for k in range(1, len(widths))], axis=...  23.4 us
  transfers between devices with their start and end apart: 4, of which 2 were waited for; matrix products, arithmetic and copies ran while one was open for 32% of the time, Pallas kernels for 0%

profile of v1, /device:TPU:1, one launch (start us, length us, event | category | flops | bytes accessed | tf_op | source)
XLA Modules:
  0.0 1010.1 jit_solution(11107434240295839737)
XLA Ops:
  11.0 109.1 %all_to_all.15 = bf16[128,8,2048]{2,1,0:T(8,128)(2,1)S(1)} all-to-all(bf16[128,8,2048]{2,1,0:T(8,128)(2,1)S(1)} %stack.2), channel_id=1, replica_groups=mesh['cp'=32,'fsdp'=4] {'cp','fsdp'}, dimensions={0} | all-to-all | bytes 8388608 | tf_op jit(solution)/shard_map/all_to_all | solution.py:95
  128.8 290.5 %all-gather.3.cloned.1.call-done = bf16[4096,2048]{0,1:T(8,128)(2,1)} async-done(((bf16[128,2048]{0,1:T(8,128)(2,1)}), bf16[4096,2048]{0,1:T(8,128)(2,1)}) %all-gather.3.cloned.1.call-update) | async-done | bytes 16777232 | tf_op jit(solution)/shard_map/all_gather | solution.py:15
  419.3 11.7 %fusion.73 = (bf16[4096,1024]{0,1:T(8,128)(2,1)}, bf16[4096,1024]{0,1:T(8,128)(2,1)}) fusion(bf16[4096,2048]{0,1:T(8,128)(2,1)} %all-gather.3.cloned.1.call-done), kind=kLoop, calls=%fused_computation.98 | loop fusion | bytes 33554432 | tf_op jit(solution)/shard_map/split | solution.py:16
  431.0 42.7 %while.60 = (s32[]{:T(128)}, f32[8,128]{1,0:T(8,128)S(1)}, f32[8,128]{1,0:T(8,128)S(1)}, s32[8]{0:T(128)S(1)}, pred[64,64]{1,0:T(8,128)(4,1)S(1)}, /*index=5*/s3...) while((s32[]{:T(128)}, f32[8,128]{1,0:T(8,128)S(1)}, ...), condition=%wide.region_3.4_spmd.clone, body=%wide.region_0.3_spmd.clone.sunk | while | flops 138023952 | bytes 8776669 | solution.py:125
  473.8 57.1 %while.61 = (s32[]{:T(128)}, f32[128,8,128]{0,2,1:T(8,128)}, s32[8]{0:T(128)S(1)}, bf16[4096,1024]{0,1:T(8,128)(2,1)}, pred[64,64]{1,0:T(8,128)(4,1)S(1)}, /*ind...) while((s32[]{:T(128)}, f32[128,8,128]{0,2,1:T(8,128)}, ...), condition=%wide.region_5.6_spmd.clone, body=%wide.region_4.5_spmd.clone.sunk | while | flops 270925856 | bytes 8661988 | solution.py:149
  535.8 8.5 all-to-all-start.1
  546.8 81.7 %while.62 = (s32[]{:T(128)}, f32[128,8,128]{0,2,1:T(8,128)}, s32[8]{0:T(128)}, bf16[4096,1024]{0,1:T(8,128)(2,1)}, pred[64,64]{1,0:T(8,128)(4,1)S(1)}, /*index=5...) while((s32[]{:T(128)}, f32[128,8,128]{0,2,1:T(8,128)}, ...), condition=%wide.region_8.9_spmd.clone, body=%wide.region_7.8_spmd.clone.sunk | while | flops 406716416 | bytes 14171124 | solution.py:184
  553.5 3.4 fusion.127
  563.6 3.5 fusion.127
  570.6 2.8 constant_dynamic-slice_fusion.14
  573.9 3.5 fusion.127
  584.1 3.5 fusion.127
  594.3 3.5 fusion.127
  604.6 3.5 fusion.127
  614.8 3.5 fusion.127
  621.8 2.8 constant_dynamic-slice_fusion.14
  625.0 3.5 fusion.127
  630.5 77.4 %all_gather.11 = f32[4096,16]{0,1:T(8,128)S(1)} all-gather(f32[128,16]{0,1:T(8,128)S(1)} %pad_maximum_fusion.2), channel_id=1, replica_groups=mesh['cp'=32,'fsdp'=4] {'cp'}, dimensions={0}, use_global_device_ids=true | all-gather | bytes 270336 | tf_op jit(solution)/shard_map/all_gather | solution.py:15
  708.0 3.8 fusion.53
  711.9 4.3 reduce_sum.70
  716.2 4.7 all-to-all-start.2
  720.9 129.7 %all-gather.5.cloned.1.call-done = bf16[4096,2048]{1,0:T(8,128)(2,1)} async-done(((bf16[128,2048]{1,0:T(8,128)(2,1)}), bf16[4096,2048]{1,0:T(8,128)(2,1)}) %all-gather.5.cloned.1.call-update) | async-done | bytes 16777232 | tf_op jit(solution)/shard_map/all_gather | solution.py:15
  850.5 11.6 %fusion.72 = (bf16[4096,1024]{1,0:T(8,128)(2,1)}, bf16[4096,1024]{1,0:T(8,128)(2,1)}) fusion(bf16[4096,2048]{1,0:T(8,128)(2,1)} %all-gather.5.cloned.1.call-done), kind=kLoop, calls=%fused_computation.97 | loop fusion | bytes 33554432 | tf_op jit(solution)/shard_map/split | solution.py:16
  862.2 135.2 %while.63 = (s32[]{:T(128)}, f32[128,8,128]{0,2,1:T(8,128)}, f32[128,8,128]{0,2,1:T(8,128)}, s32[8]{0:T(128)S(1)}, bf16[4096,1024]{1,0:T(8,128)(2,1)}, /*index=5...) while((s32[]{:T(128)}, f32[128,8,128]{0,2,1:T(8,128)}, ...), condition=%wide.region_12.13_spmd.clone, body=%wide.region_9.12_spmd.clone.sunk | while | flops 544604160 | bytes 51485988 | solution.py:228
  (688 shorter events, 286.3 us)
Async XLA Ops:
  7.2 115.0 %copy-start = (bf16[1,128,2048]{2,1,0:T(8,128)(2,1)S(1)}, bf16[1,128,2048]{2,1,0:T(8,128)(2,1)}, u32[]{:S(2)}) copy-start(bf16[1,128,2048]{2,1,0:T(8,128)(2,1)} %param.21) | copy-start | bytes 1572868
  7.2 3.3 copy-start.16
  7.2 412.1 %all-gather.3.cloned.1.call-start = ((), (), s32[]{:S(2)}) async-start(), calls=%async_computation.3 | async-start | bytes 17301504 | tf_op jit(solution)/shard_map/all_gather | solution.py:15
  10.4 840.1 %all-gather.5.cloned.1.call-start = ((), (), s32[]{:S(2)}) async-start(), calls=%async_computation.4 | async-start | bytes 17301504 | tf_op jit(solution)/shard_map/all_gather | solution.py:15
  122.1 4.1 copy-start.17
  122.1 4.1 copy-start.18
  532.1 12.2 %copy-start.11 = (bf16[128,1024]{1,0:T(8,128)(2,1)}, bf16[128,1024]{1,0:T(8,128)(2,1)S(1)}, u32[]{:S(2)}) copy-start(bf16[128,1024]{1,0:T(8,128)(2,1)S(1)} %copy.212) | copy-start | bytes 786436
  535.8 176.1 %all-to-all-start.1 = ((bf16[4,256,2048]{2,1,0:T(8,128)(2,1)}), bf16[4,256,2048]{2,1,0:T(8,128)(2,1)}, u32[]{:S(2)}, u32[]{:S(2)}) async-start(bf16[4,256,2048]{2,1,0:T(8,128)(2,1)} %bitcast.268), calls=%async_computation.1 | async-start | bytes 8388608 | tf_op jit(solution)/shard_map/all_to_all | solution.py:26
  716.2 285.1 %all-to-all-start.2 = ((bf16[32,8,2048]{2,1,0:T(8,128)(2,1)}), bf16[32,8,2048]{2,1,0:T(8,128)(2,1)}, u32[]{:S(2)}, u32[]{:S(2)}) async-start(bf16[32,8,2048]{2,1,0:T(8,128)(2,1)} %bitcast.18), calls=%async_computation.2 | async-start | bytes 2097152 | tf_op jit(solution)/shard_map/all_to_all | solution.py:26
  720.8 141.3 %copy-start.9 = (bf16[1,128,1024]{2,1,0:T(8,128)(2,1)S(1)}, bf16[1,128,1024]{2,1,0:T(8,128)(2,1)}, u32[]{:S(2)}) copy-start(bf16[1,128,1024]{2,1,0:T(8,128)(2,1)} %param.17) | copy-start | bytes 786436
  862.2 2.8 copy-start.12
  862.2 2.8 copy-start.14
  879.1 2.8 copy-start.12
  879.1 2.8 copy-start.14
  896.0 2.8 copy-start.12
  896.0 2.8 copy-start.14
  912.9 2.8 copy-start.12
  912.9 2.8 copy-start.14
  929.8 2.8 copy-start.12
  929.8 2.8 copy-start.14
  946.6 2.8 copy-start.12
  946.7 2.8 copy-start.14
  963.5 2.8 copy-start.12
  997.3 6.0 copy-start.1
  (69 other events, 110.5 us)
Sparse Core Ops, SparseCore 0:
  10.5 408.7 all-gather.2
  421.0 429.5 all-gather.4
